TPU v7x, 32 devices: a whole 2x2x4 slice. The times are simulated.
32 devices in a mesh: horiz: 8 (over z, y), depth: 4 (over x, core).
Axes of the slice: x: 2, y: 2, z: 4, core: 2. Of those that a mesh axis runs over, the one named last changes fastest.
Arguments:
- adjoint_state: float32 [9, 32, 128, 128], P(None, 'depth', 'horiz'), may hold values from -6 to 6
- buoyancy: float32 [32, 128, 128], P('depth', 'horiz'), may hold values from 0.5 to 1
- lame_lambda: float32 [32, 128, 128], P('depth', 'horiz'), may hold values from 0.5 to 1.5
- shear_modulus: float32 [32, 128, 128], P('depth', 'horiz'), may hold values from 0.3 to 1
- forward_field: float32 [32, 128, 128], P('depth', 'horiz'), may hold values from -6 to 6
- traces: float32 [256, 32, 128], P('horiz', 'depth'), may hold values from -6 to 6
- observed: float32 [4, 2, 512, 256], P('depth', None, 'horiz'), may hold values from -6 to 6
- pairs: int32 [256, 2], replicated, may hold values from 0 to 255
- patch_basis: float32 [16, 128], P(None, 'horiz'), may hold values from -0.375 to 0.375
- patch_ids: int32 [8, 16], P('horiz'), may hold values from 0 to 31, as said below
- slot_counts: int32 [8], P('horiz'), may hold values from 8 to 16, as said below
- owner_map: int32 [32], replicated, may hold values from 0 to 7, as said below
Outputs:
- adjoint_final: float32 [9, 32, 128, 128], P(None, 'depth', 'horiz')
- cross_spectra: float32 [4, 2, 512, 256], P('depth', None, 'horiz')
- patch_grad: float32 [4, 64, 128], P('depth', 'horiz')
Inputs may be any that keep to these rules, and one draw needn't show every extreme that they name: Tile h uses its first slot_counts[h] slots; some tile uses all 16. `patch_ids`: the patches named in one tile are distinct; among the used slots of one tile at most 2 name patches of one owner, and some tile reaches 2. `owner_map`: every owner holds 2 or more patches and at most 8; some owner holds exactly 8.
All inputs are finite; a program needn't handle non-finite values.
Results may differ from a plain program's by a relative error of at most 0.00012.
Values sent between devices are 32-bit elements; how exact they have to be, the bound alone decides.
A program may use at most 64 MiB of HBM per device.

v0:
```python
import functools
import math

import jax
import jax.numpy as jnp
import numpy as np
from jax import lax
from jax.experimental import pallas as pl
from jax.experimental.pallas import tpu as pltpu
from jax.sharding import PartitionSpec as P

ITERS = 4
CAP = 2
OWN_CAP = 8


time_step = 0.25
precise_mode = lax.Precision.HIGHEST


def with_halo(cells, sides, width):
    for axis, dim in sides:
        count = lax.axis_size(axis)
        ends = count - 1
        head = lax.slice_in_dim(cells, 0, width, axis=dim)
        tail = lax.slice_in_dim(cells, cells.shape[dim] - width, cells.shape[dim], axis=dim)
        cells = jnp.concatenate(
            [
                lax.ppermute(tail, axis, [(i, (i + 1) % count) for i in range(ends)]),
                cells,
                lax.ppermute(head, axis, [((i + 1) % count, i) for i in range(ends)]),
            ],
            axis=dim,
        )
    return cells


def forward_diff(field, along):
    extent = field.shape[along]
    ahead = jnp.concatenate(
        [
            lax.slice_in_dim(field, 1, extent, axis=along),
            jnp.zeros_like(lax.slice_in_dim(field, 0, 1, axis=along)),
        ],
        axis=along,
    )
    return ahead - field


def backward_diff(field, along):
    extent = field.shape[along]
    behind = jnp.concatenate(
        [
            jnp.zeros_like(lax.slice_in_dim(field, 0, 1, axis=along)),
            lax.slice_in_dim(field, 0, extent - 1, axis=along),
        ],
        axis=along,
    )
    return field - behind


def ahead_z(padded):
    return padded[2:, 1:-1] - padded[1:-1, 1:-1]


def behind_z(padded):
    return padded[1:-1, 1:-1] - padded[:-2, 1:-1]


def ahead_x(padded):
    return padded[1:-1, 2:] - padded[1:-1, 1:-1]


def behind_x(padded):
    return padded[1:-1, 1:-1] - padded[1:-1, :-2]


def update_stresses(
    vel_x,
    vel_y,
    vel_z,
    str_xx,
    str_yy,
    str_zz,
    str_xy,
    str_xz,
    str_yz,
    strain_xx,
    strain_zz,
    vx_ahead_z,
    vy_ahead_x,
    vy_ahead_z,
    vz_ahead_x,
    lame_lambda,
    shear_modulus,
):
    strain_yy = backward_diff(vel_y, 2)
    p_modulus = lame_lambda + 2.0 * shear_modulus
    str_xx = str_xx + time_step * (p_modulus * strain_xx + lame_lambda * (strain_yy + strain_zz))
    str_yy = str_yy + time_step * (p_modulus * strain_yy + lame_lambda * (strain_xx + strain_zz))
    str_zz = str_zz + time_step * (p_modulus * strain_zz + lame_lambda * (strain_xx + strain_yy))
    str_xy = str_xy + time_step * shear_modulus * (forward_diff(vel_x, 2) + vy_ahead_x)
    str_xz = str_xz + time_step * shear_modulus * (vx_ahead_z + vz_ahead_x)
    str_yz = str_yz + time_step * shear_modulus * (vy_ahead_z + forward_diff(vel_z, 2))
    return [vel_x, vel_y, vel_z, str_xx, str_yy, str_zz, str_xy, str_xz, str_yz]


def leapfrog(fields, buoyancy, lame_lambda, shear_modulus):
    vel_x, vel_y, vel_z, str_xx, str_yy, str_zz, str_xy, str_xz, str_yz = fields
    stress_pad = with_halo(
        jnp.stack([str_xx, str_zz, str_xy, str_xz, str_yz]), (("horiz", 2), ("depth", 1)), 1
    )
    vel_x = vel_x + time_step * buoyancy * (
        ahead_x(stress_pad[0]) + backward_diff(str_xy, 2) + behind_z(stress_pad[3])
    )
    vel_y = vel_y + time_step * buoyancy * (
        behind_x(stress_pad[2]) + forward_diff(str_yy, 2) + behind_z(stress_pad[4])
    )
    vel_z = vel_z + time_step * buoyancy * (
        behind_x(stress_pad[3]) + backward_diff(str_yz, 2) + ahead_z(stress_pad[1])
    )
    velocity_pad = with_halo(jnp.stack([vel_x, vel_y, vel_z]), (("horiz", 2), ("depth", 1)), 1)
    return update_stresses(
        vel_x,
        vel_y,
        vel_z,
        str_xx,
        str_yy,
        str_zz,
        str_xy,
        str_xz,
        str_yz,
        behind_x(velocity_pad[0]),
        behind_z(velocity_pad[2]),
        ahead_z(velocity_pad[0]),
        ahead_x(velocity_pad[1]),
        ahead_z(velocity_pad[1]),
        ahead_x(velocity_pad[2]),
        lame_lambda,
        shear_modulus,
    )


def shards(
    adjoint_state,
    buoyancy,
    lame_lambda,
    shear_modulus,
    forward_field,
    traces,
    observed,
    pairs,
    patch_basis,
    patch_ids,
    slot_counts,
    owner_map,
):
    local_stations, local_blocks, samples = traces.shape
    bin_count = samples // 2
    tile_count = lax.axis_size("horiz")
    slab_count = lax.axis_size("depth")
    tile_index = lax.axis_index("horiz")
    depth_index = lax.axis_index("depth")
    stations = local_stations * tile_count
    group_items = local_blocks * bin_count
    items_dev = group_items // tile_count
    n_pairs = pairs.shape[0]
    x_cells = forward_field.shape[1]
    y_cells = forward_field.shape[2]
    sample_index = lax.iota(jnp.int32, samples)
    frequency = lax.iota(jnp.int32, bin_count) + 1
    phases = sample_index[:, None] * frequency[None, :] % samples
    angles = phases.astype(jnp.float32) * (2.0 * math.pi / samples)
    fourier_table = jnp.concatenate([jnp.cos(angles), -jnp.sin(angles)], axis=1) / math.sqrt(
        samples
    )
    spectra = jnp.einsum("sbt,tm->mbs", traces, fourier_table, precision=precise_mode)
    spectra = spectra.reshape(2, tile_count, items_dev, local_stations)
    first_station = pairs[:, 0]
    second_station = pairs[:, 1]
    received_block = lax.all_to_all(spectra, "horiz", split_axis=1, concat_axis=3, tiled=True)[:, 0]
    first_spec = jnp.take(received_block, first_station, axis=2)
    second_spec = jnp.take(received_block, second_station, axis=2)
    cross_real = first_spec[0] * second_spec[0] + first_spec[1] * second_spec[1]
    cross_imag = first_spec[0] * second_spec[1] - first_spec[1] * second_spec[0]
    cross = jnp.stack([cross_real, cross_imag])
    items_all = group_items * slab_count
    positions = (
        depth_index * group_items + tile_index * items_dev + lax.iota(jnp.int32, items_dev)
    ).astype(jnp.float32)
    weights = 1.0 + 2.0 * positions / (items_all - 1)
    deviation = cross - observed[0]
    pair_terms = jnp.sum(weights[None, :, None] * deviation * deviation, axis=(0, 1)) / (
        2.0 * items_all
    )
    all_terms = lax.psum(pair_terms, ("horiz", "depth"))
    total_all = jax.ops.segment_sum(all_terms, first_station, stations) + jax.ops.segment_sum(
        all_terms, second_station, stations
    )
    station_total = lax.dynamic_slice_in_dim(total_all, tile_index * local_stations, local_stations)
    unit_terms = jnp.ones((n_pairs,), jnp.float32)
    count_all = jax.ops.segment_sum(unit_terms, first_station, stations) + jax.ops.segment_sum(
        unit_terms, second_station, stations
    )
    station_count = lax.dynamic_slice_in_dim(count_all, tile_index * local_stations, local_stations)
    station_weight = station_total / jnp.maximum(station_count, 1.0)
    station_slot = lax.iota(jnp.int32, local_stations)
    onehot_x = ((station_slot % x_cells)[:, None] == lax.iota(jnp.int32, x_cells)[None, :]).astype(
        jnp.float32
    )
    onehot_y = (
        (53 * station_slot % y_cells)[:, None] == lax.iota(jnp.int32, y_cells)[None, :]
    ).astype(jnp.float32)
    deposit = jnp.dot((station_weight[:, None] * onehot_x).T, onehot_y, precision=precise_mode)
    surface = (depth_index == 0).astype(jnp.float32)
    fields = list(adjoint_state)
    fields[2] = fields[2].at[0].add(surface * deposit)
    for iteration in range(ITERS):
        fields = leapfrog(fields, buoyancy, lame_lambda, shear_modulus)
    adjoint_final = jnp.stack(fields)
    kernel = jnp.sum(fields[2] * forward_field, axis=0)
    slot_rows = jnp.dot(patch_basis, kernel, precision=precise_mode)
    n_slots = patch_ids.shape[1]
    n_patch = owner_map.shape[0]
    slot_used = lax.iota(jnp.int32, n_slots) < slot_counts[0]
    slot_ids = patch_ids[0]
    patch_order = lax.iota(jnp.int32, n_patch)
    same_owner = owner_map[:, None] == owner_map[None, :]
    earlier = patch_order[None, :] < patch_order[:, None]
    patch_rank = jnp.sum((same_owner & earlier).astype(jnp.int32), axis=1)
    rank_slots = lax.iota(jnp.int32, OWN_CAP)
    target = owner_map[slot_ids]
    dest_hot = (
        (target[:, None] == lax.iota(jnp.int32, tile_count)[None, :]) & slot_used[:, None]
    ).astype(jnp.int32)
    running = jnp.cumsum(dest_hot, axis=0) - 1
    position = jnp.sum(dest_hot * running, axis=1)
    buffer_index = target * CAP + position
    selector = (
        lax.iota(jnp.int32, tile_count * CAP)[:, None] == buffer_index[None, :]
    ) & slot_used[None, :]
    send_rows = jnp.dot(selector.astype(jnp.float32), slot_rows, precision=precise_mode).reshape(
        tile_count, CAP, y_cells
    )
    send_ids = jnp.sum(jnp.where(selector, slot_ids[None, :], 0), axis=1).reshape(tile_count, CAP)
    got_rows, got_ids = (
        lax.all_to_all(send_rows, "horiz", split_axis=0, concat_axis=0, tiled=True),
        lax.all_to_all(send_ids, "horiz", split_axis=0, concat_axis=0, tiled=True),
    )
    got_rows = got_rows.reshape(tile_count * CAP, y_cells)
    got_ids = got_ids.reshape(tile_count * CAP)
    placing = (
        (patch_rank[got_ids][None, :] == rank_slots[:, None])
        & (owner_map[got_ids] == tile_index)[None, :]
    ).astype(jnp.float32)
    patch_grad = jnp.dot(placing, got_rows, precision=precise_mode)
    return (adjoint_final, cross[None], patch_grad[None])


LEV, XC, YC, STN, BLK, FREQ = 8, 16, 128, 32, 8, 8
VX, VY, VZ, SXX, SYY, SZZ, SXY, SXZ, SYZ, BUO, LAM, MU = range(12)
EXT_X = XC + 8
FIRST = 5
CHUNKS = 6
MESH = pl.DeviceIdType.MESH


def split3(value):
    high = value.astype(jnp.bfloat16)
    rest = value - high.astype(jnp.float32)
    mid = rest.astype(jnp.bfloat16)
    low = (rest - mid.astype(jnp.float32)).astype(jnp.bfloat16)
    return high, mid, low


def dot32(a, b, dims):
    return lax.dot_general(
        a, b, (dims, ((), ())), precision=precise_mode, preferred_element_type=jnp.float32
    )


def roll_x(f, up):
    return pltpu.roll(f, EXT_X - 1 if up else 1, 0)


def velocity_levels(ext, mats, first, count):
    lane = lax.broadcasted_iota(jnp.int32, (EXT_X, YC), 1)

    def ahead_y(f):
        return jnp.where(lane == YC - 1, 0.0, pltpu.roll(f, YC - 1, 1)) - f

    def behind_y(f):
        return f - jnp.where(lane == 0, 0.0, pltpu.roll(f, 1, 1))

    results = []
    for i in range(count):
        z = first + i
        sxy = ext[SXY, z]
        sxz = ext[SXZ, z]
        syz = ext[SYZ, z]
        sxx = ext[SXX, z]
        scale = time_step * mats[BUO, z]
        vx = ext[VX, z] + scale * (
            (roll_x(sxx, True) - sxx) + behind_y(sxy) + (sxz - ext[SXZ, z - 1])
        )
        vy = ext[VY, z] + scale * (
            (sxy - roll_x(sxy, False)) + ahead_y(ext[SYY, z]) + (syz - ext[SYZ, z - 1])
        )
        vz = ext[VZ, z] + scale * (
            (sxz - roll_x(sxz, False)) + behind_y(syz) + (ext[SZZ, z + 1] - ext[SZZ, z])
        )
        results.append((vx, vy, vz))
    for i in range(count):
        for k, value in zip((VX, VY, VZ), results[i]):
            ext[k, first + i] = value


def stress_levels(ext, mats, first, count):
    lane = lax.broadcasted_iota(jnp.int32, (EXT_X, YC), 1)

    def ahead_y(f):
        return jnp.where(lane == YC - 1, 0.0, pltpu.roll(f, YC - 1, 1)) - f

    def behind_y(f):
        return f - jnp.where(lane == 0, 0.0, pltpu.roll(f, 1, 1))

    results = []
    for i in range(count):
        z = first + i
        vx = ext[VX, z]
        vy = ext[VY, z]
        vz = ext[VZ, z]
        lam = time_step * mats[LAM, z]
        mu = time_step * mats[MU, z]
        exx = vx - roll_x(vx, False)
        eyy = behind_y(vy)
        ezz = vz - ext[VZ, z - 1]
        p_mod = lam + 2.0 * mu
        sxx = ext[SXX, z] + (p_mod * exx + lam * (eyy + ezz))
        syy = ext[SYY, z] + (p_mod * eyy + lam * (exx + ezz))
        szz = ext[SZZ, z] + (p_mod * ezz + lam * (exx + eyy))
        sxy = ext[SXY, z] + mu * (ahead_y(vx) + (roll_x(vy, True) - vy))
        sxz = ext[SXZ, z] + mu * ((ext[VX, z + 1] - vx) + (roll_x(vz, True) - vz))
        syz = ext[SYZ, z] + mu * ((ext[VY, z + 1] - vy) + ahead_y(vz))
        results.append((sxx, syy, szz, sxy, sxz, syz))
    for i in range(count):
        for k, value in zip((SXX, SYY, SZZ, SXY, SXZ, SYZ), results[i]):
            ext[k, first + i] = value


def fused_kernel(
    tiles,
    slabs,
    state_ref,
    buo_ref,
    lam_ref,
    mu_ref,
    forward_ref,
    traces_ref,
    observed_ref,
    pairs_ref,
    basis_ref,
    ids_ref,
    counts_ref,
    owner_ref,
    table_ref,
    final_ref,
    cross_ref,
    grad_ref,
    ext,
    pack_r,
    pack_l,
    halo_r,
    halo_l,
    spec_out,
    spec_in,
    left_rows,
    right_rows,
    part,
    parts,
    added,
    rows_out,
    rows_in,
    local_sem,
    spec_send,
    spec_recv,
    slab_send,
    slab_recv,
    side_send,
    side_recv,
    corner_send,
    corner_recv,
    part_send,
    part_recv,
    row_send,
    row_recv,
):
    me = lax.axis_index("horiz")
    depth = lax.axis_index("depth")
    n_pairs = pairs_ref.shape[1]
    own = pl.ds(FIRST, LEV)
    arrays = ((0, 9, state_ref), (9, 1, buo_ref), (10, 1, lam_ref), (11, 1, mu_ref))

    locals_in = [
        pltpu.make_async_copy(
            src, ext.at[pl.ds(start, count), own, pl.ds(0, XC)], local_sem.at[n]
        )
        for n, (start, count, src) in enumerate(arrays)
    ]
    for copy in locals_in:
        copy.start()

    barrier = pltpu.get_barrier_semaphore()
    for d in range(slabs):
        for k in range(tiles):
            if d or k:
                other = {"horiz": lax.rem(me + k, tiles), "depth": lax.rem(depth + d, slabs)}
                pl.semaphore_signal(barrier, inc=1, device_id=other, device_id_type=MESH)

    by_block = jnp.concatenate(
        [traces_ref[pl.ds(b, STN, stride=BLK), :] for b in range(BLK)], axis=0
    )
    spectra = dot32(table_ref[...], by_block, ((1,), (1,)))
    half = tiles * FREQ
    for t in range(tiles):
        for c in range(2):
            spec_out[t, pl.ds(c * FREQ, FREQ), :] = spectra[
                c * half + t * FREQ : c * half + (t + 1) * FREQ
            ]

    pl.semaphore_wait(barrier, tiles * slabs - 1)

    spec_copies = []
    for k in range(1, tiles):
        peer = lax.rem(me + k, tiles)
        spec_copies.append(
            pltpu.make_async_remote_copy(
                src_ref=spec_out.at[peer],
                dst_ref=spec_in.at[me],
                send_sem=spec_send.at[k],
                recv_sem=spec_recv.at[k],
                device_id={"horiz": peer},
                device_id_type=MESH,
            )
        )
    for copy in spec_copies:
        copy.start()
    spec_in[me] = spec_out[me]

    row = lax.broadcasted_iota(jnp.int32, (8, YC), 0)
    lower = row < 4
    for copy in locals_in:
        copy.wait()

    def pack_one(a, carry):
        for j in range(LEV // 2):
            even, odd = FIRST + 2 * j, FIRST + 2 * j + 1
            pack_r[a, j] = jnp.where(
                lower, ext[a, even, pl.ds(0, 8)], pltpu.roll(ext[a, odd, pl.ds(0, 8)], 4, 0)
            )
            pack_l[a, j] = jnp.where(
                lower, pltpu.roll(ext[a, odd, pl.ds(8, 8)], 4, 0), ext[a, even, pl.ds(8, 8)]
            )
        return carry

    lax.fori_loop(0, 12, pack_one, 0)

    mid_pairs = pl.ds(2, LEV // 2)

    def side_copy(n, c):
        source, target, step = ((pack_r, halo_r, -1), (pack_l, halo_l, 1))[n]
        some = pl.ds(c * 12 // CHUNKS, 12 // CHUNKS)
        return pltpu.make_async_remote_copy(
            src_ref=source.at[some],
            dst_ref=target.at[some, mid_pairs],
            send_sem=side_send.at[n, c],
            recv_sem=side_recv.at[n, c],
            device_id={"horiz": me + step},
            device_id_type=MESH,
        )

    def slab_copy(n, m):
        start, count, src = arrays[m]
        levels = pl.ds(0, 4) if n == 0 else pl.ds(LEV - 4, 4)
        source = src.at[:, levels]
        target = ext.at[
            pl.ds(start, count), pl.ds(FIRST + LEV if n == 0 else FIRST - 4, 4), pl.ds(0, XC)
        ]
        return pltpu.make_async_remote_copy(
            src_ref=source,
            dst_ref=target,
            send_sem=slab_send.at[n, m],
            recv_sem=slab_recv.at[n, m],
            device_id={"depth": depth + (-1 if n == 0 else 1)},
            device_id_type=MESH,
        )

    def corner_copy(n, m, c):
        buffer = (halo_r, halo_l)[m]
        some = pl.ds(c * 12 // CHUNKS, 12 // CHUNKS)
        return pltpu.make_async_remote_copy(
            src_ref=buffer.at[some, pl.ds(2 if n == 0 else 4, 2)],
            dst_ref=buffer.at[some, pl.ds(6 if n == 0 else 0, 2)],
            send_sem=corner_send.at[n, m, c],
            recv_sem=corner_recv.at[n, m, c],
            device_id={"depth": depth + (-1 if n == 0 else 1)},
            device_id_type=MESH,
        )

    has_left, has_right = me > 0, me < tiles - 1
    has_up, has_down = depth > 0, depth < slabs - 1

    for c in range(CHUNKS):

        @pl.when(has_left)
        def _():
            side_copy(0, c).start()

        @pl.when(has_right)
        def _():
            side_copy(1, c).start()

    @pl.when(has_up)
    def _():
        for m in range(4):
            slab_copy(0, m).start()

    @pl.when(has_down)
    def _():
        for m in range(4):
            slab_copy(1, m).start()

    def clear_levels(first):
        def clear(a, carry):
            for i in range(4):
                ext[a, first + i] = jnp.zeros((EXT_X, YC), jnp.float32)
            return carry

        lax.fori_loop(0, 12, clear, 0)

    def clear_pairs(buffer, first, count):
        def clear(a, carry):
            for i in range(count):
                buffer[a, first + i] = jnp.zeros((8, YC), jnp.float32)
            return carry

        lax.fori_loop(0, 12, clear, 0)

    @pl.when(jnp.logical_not(has_up))
    def _():
        clear_levels(FIRST - 4)
        clear_pairs(halo_r, 0, 2)
        clear_pairs(halo_l, 0, 2)

    @pl.when(jnp.logical_not(has_down))
    def _():
        clear_levels(FIRST + LEV)
        clear_pairs(halo_r, 6, 2)
        clear_pairs(halo_l, 6, 2)

    @pl.when(jnp.logical_not(has_right))
    def _():
        clear_pairs(halo_r, 2, 4)

    @pl.when(jnp.logical_not(has_left))
    def _():
        clear_pairs(halo_l, 2, 4)

    def clear_ends(a, carry):
        ext[a, 0] = jnp.zeros((EXT_X, YC), jnp.float32)
        ext[a, 17] = jnp.zeros((EXT_X, YC), jnp.float32)
        return carry

    lax.fori_loop(0, 12, clear_ends, 0)

    def clear_added(a, carry):
        for i in range(ITERS + 3):
            added[a, FIRST - 1 + i] = jnp.zeros((EXT_X, YC), jnp.float32)
        return carry

    @pl.when(depth == 0)
    def _():
        lax.fori_loop(0, 9, clear_added, 0)

    first_pair = pairs_ref[pl.ds(0, 1), :]
    second_pair = pairs_ref[pl.ds(1, 1), :]
    stations = tiles * STN
    station = lax.broadcasted_iota(jnp.int32, (stations, n_pairs), 0)
    hot_first = (station == first_pair).astype(jnp.float32).astype(jnp.bfloat16)
    hot_second = (station == second_pair).astype(jnp.float32).astype(jnp.bfloat16)
    n_patch = owner_ref.shape[1]
    n_slots = ids_ref.shape[1]
    owner_row = owner_ref[...]
    up_iota = lax.broadcasted_iota(jnp.int32, (n_patch, n_patch), 0)
    across = lax.broadcasted_iota(jnp.int32, (n_patch, n_patch), 1)
    owner_wide = jnp.broadcast_to(owner_row, (n_patch, n_patch))
    owner_col = jnp.sum(jnp.where(up_iota == across, owner_wide, 0), axis=1, keepdims=True)
    rank_row = jnp.sum(
        jnp.where((owner_col == owner_wide) & (up_iota < across), 1, 0), axis=0, keepdims=True
    )
    target_row = owner_row * OWN_CAP + rank_row
    out_rows = tiles * OWN_CAP
    place = (
        lax.broadcasted_iota(jnp.int32, (out_rows, n_patch), 0) == target_row
    ).astype(jnp.float32)
    slot = lax.broadcasted_iota(jnp.int32, (n_patch, n_slots), 1)
    patch = lax.broadcasted_iota(jnp.int32, (n_patch, n_slots), 0)
    named = ((patch == ids_ref[...]) & (slot < counts_ref[...])).astype(jnp.float32)
    slot_place = dot32(place, named, ((1,), (0,)))
    row_basis = dot32(slot_place, basis_ref[...], ((1,), (0,)))

    for copy in spec_copies:
        copy.wait_recv()
    for b in range(BLK):
        wide = jnp.concatenate(
            [spec_in[t][:, b * STN : (b + 1) * STN] for t in range(tiles)], axis=1
        )
        left_rows[pl.ds(b * 2 * FREQ, 2 * FREQ), :] = wide[:, :128]
        right_rows[pl.ds(b * 2 * FREQ, 2 * FREQ), :] = wide[:, 128:]
    ordered = jnp.concatenate(
        [
            jnp.concatenate(
                [r[pl.ds(cf, BLK, stride=2 * FREQ), :] for cf in range(2 * FREQ)], axis=0
            )
            for r in (left_rows, right_rows)
        ],
        axis=1,
    )
    pieces = split3(ordered)

    def gather(hot):
        return sum(
            lax.dot_general(
                piece, hot, (((1,), (0,)), ((), ())), preferred_element_type=jnp.float32
            )
            for piece in pieces[::-1]
        )

    first_spec = gather(hot_first)
    second_spec = gather(hot_second)
    items = FREQ * BLK
    f_re, f_im = first_spec[:items], first_spec[items:]
    s_re, s_im = second_spec[:items], second_spec[items:]
    cross_re = f_re * s_re + f_im * s_im
    cross_im = f_re * s_im - f_im * s_re
    items_all = items * tiles * slabs
    item = lax.broadcasted_iota(jnp.int32, (items, 1), 0) + (depth * tiles + me) * items
    weight = 1.0 + 2.0 * item.astype(jnp.float32) / (items_all - 1)
    dev_re = cross_re - observed_ref[0, 0]
    dev_im = cross_im - observed_ref[0, 1]
    terms = weight * (dev_re * dev_re + dev_im * dev_im)
    part[...] = jnp.sum(terms, axis=0, keepdims=True)

    def part_copy(d, k, receiving=False):
        slot = d * tiles + (lax.rem(me + tiles - k, tiles) if receiving else me)
        return pltpu.make_async_remote_copy(
            src_ref=part,
            dst_ref=parts.at[slot],
            send_sem=part_send.at[k],
            recv_sem=part_recv.at[d, k],
            device_id={"horiz": lax.rem(me + k, tiles), "depth": 0},
            device_id_type=MESH,
        )

    for k in range(1, tiles):
        part_copy(depth, k).start()

    @pl.when(depth > 0)
    def _():
        part_copy(depth, 0).start()

    cross_ref[0, 0] = cross_re
    cross_ref[0, 1] = cross_im

    for c in range(CHUNKS):

        @pl.when(has_left)
        def _():
            side_copy(1, c).wait_recv()

        @pl.when(has_right)
        def _():
            side_copy(0, c).wait_recv()

        @pl.when(has_up)
        def _():
            for m in range(2):
                corner_copy(0, m, c).start()

        @pl.when(has_down)
        def _():
            for m in range(2):
                corner_copy(1, m, c).start()

    def unpack(first, count):
        def unpack_one(a, carry):
            for j in range(first, first + count):
                r, l = halo_r[a, j], halo_l[a, j]
                ext[a, 1 + 2 * j, pl.ds(XC, 8)] = jnp.where(lower, r, l)
                ext[a, 2 + 2 * j, pl.ds(XC, 8)] = pltpu.roll(jnp.where(lower, l, r), 4, 0)
            return carry

        lax.fori_loop(0, 12, unpack_one, 0)

    unpack(2, 4)

    @pl.when(has_up)
    def _():
        for m in range(4):
            slab_copy(1, m).wait_recv()
        for m in range(2):
            for c in range(CHUNKS):
                corner_copy(1, m, c).wait_recv()

    @pl.when(has_down)
    def _():
        for m in range(4):
            slab_copy(0, m).wait_recv()
        for m in range(2):
            for c in range(CHUNKS):
                corner_copy(0, m, c).wait_recv()

    unpack(0, 2)
    unpack(6, 2)

    for n in range(ITERS):

        def v_body(i, carry):
            velocity_levels(ext, ext, 1 + n + 2 * i, 2)
            return carry

        def s_body(i, carry):
            stress_levels(ext, ext, 2 + n + 2 * i, 2)
            return carry

        lax.fori_loop(0, 8 - n, v_body, 0)
        lax.fori_loop(0, 7 - n, s_body, 0)

    @pl.when(depth == 0)
    def _():
        for d in range(slabs):
            for k in range(tiles):
                if d or k:
                    part_copy(d, k, True).wait_recv()
        parts[me] = part[...]
        total = parts[0]
        for t in range(1, tiles * slabs):
            total = total + parts[t]
        terms = total / (2.0 * items_all)
        ext_row = lax.broadcasted_iota(jnp.int32, (EXT_X, 1), 0)
        x = me * XC + jnp.where(ext_row < XC + 4, ext_row, ext_row - EXT_X)
        x_pos = x + XC
        tile = x_pos // XC - 1
        in_tile = x_pos - (tile + 1) * XC
        lane = lax.broadcasted_iota(jnp.int32, (EXT_X, YC), 1)
        deposit = jnp.zeros((EXT_X, YC), jnp.float32)
        for turn in range(STN // XC):
            within = in_tile + turn * XC
            index = tile * STN + within
            hits = (index == first_pair).astype(jnp.float32) + (index == second_pair).astype(
                jnp.float32
            )
            sums = jnp.sum(hits * terms, axis=1, keepdims=True)
            number = jnp.sum(hits, axis=1, keepdims=True)
            value = sums / jnp.maximum(number, 1.0)
            deposit = deposit + jnp.where(lane == lax.rem(53 * within, YC), value, 0.0)
        added[VZ, FIRST] = deposit
        for n in range(ITERS):
            if n:
                for z in range(0, n + 1, 2):
                    velocity_levels(added, ext, FIRST + z, min(2, n + 1 - z))
            for z in range(0, n + 2, 2):
                stress_levels(added, ext, FIRST + z, min(2, n + 2 - z))

        def add_one(a, carry):
            for i in range(ITERS + 1):
                ext[a, FIRST + i, pl.ds(0, XC)] += added[a, FIRST + i, pl.ds(0, XC)]
            return carry

        lax.fori_loop(0, 9, add_one, 0)

    final = pltpu.make_async_copy(
        ext.at[pl.ds(0, 9), own, pl.ds(0, XC)], final_ref, local_sem.at[4]
    )
    final.start()
    slab = sum(ext[VZ, FIRST + i, pl.ds(0, XC)] * forward_ref[i] for i in range(LEV))
    rows = dot32(row_basis, slab, ((1,), (0,)))
    for t in range(tiles):
        rows_out[t] = rows[t * OWN_CAP : (t + 1) * OWN_CAP]
    row_copies = []
    for k in range(1, tiles):
        peer = lax.rem(me + k, tiles)
        row_copies.append(
            pltpu.make_async_remote_copy(
                src_ref=rows_out.at[peer],
                dst_ref=rows_in.at[me],
                send_sem=row_send.at[k],
                recv_sem=row_recv.at[k],
                device_id={"horiz": peer},
                device_id_type=MESH,
            )
        )
    for copy in row_copies:
        copy.start()
    rows_in[me] = rows_out[me]

    for copy in spec_copies:
        copy.wait_send()

    @pl.when(has_left)
    def _():
        for c in range(CHUNKS):
            side_copy(0, c).wait_send()

    @pl.when(has_right)
    def _():
        for c in range(CHUNKS):
            side_copy(1, c).wait_send()

    @pl.when(has_up)
    def _():
        for m in range(4):
            slab_copy(0, m).wait_send()
        for m in range(2):
            for c in range(CHUNKS):
                corner_copy(0, m, c).wait_send()

    @pl.when(has_down)
    def _():
        for m in range(4):
            slab_copy(1, m).wait_send()
        for m in range(2):
            for c in range(CHUNKS):
                corner_copy(1, m, c).wait_send()

    for k in range(1, tiles):
        part_copy(depth, k).wait_send()

    @pl.when(depth > 0)
    def _():
        part_copy(depth, 0).wait_send()

    for copy in row_copies:
        copy.wait_recv()
    grad_ref[0] = sum(rows_in[t] for t in range(tiles))
    for copy in row_copies:
        copy.wait_send()
    final.wait()


def hand_out_kernel(*refs):
    sources, results, buffers = refs[:3], refs[3:6], refs[6:9]
    in_sem, out_sem = refs[9:]
    fields = sources[0].shape[0]
    moves = [(0, pl.ds(n, 1)) for n in range(fields)] + [(1, pl.ds(0, 1)), (2, pl.ds(0, 1))]
    reads, writes = [], []
    for n, (k, some) in enumerate(moves):
        reads.append(
            pltpu.make_async_copy(sources[k].at[some], buffers[k].at[some], in_sem.at[n])
        )
        writes.append(
            pltpu.make_async_copy(buffers[k].at[some], results[k].at[some], out_sem.at[n])
        )
        reads[-1].start()
    for read, write in zip(reads, writes):
        read.wait()
        write.start()
    for write in writes:
        write.wait()


def hand_out(*arrays):
    shapes = [jax.ShapeDtypeStruct(a.shape, a.dtype) for a in arrays]
    anywhere = pl.BlockSpec(memory_space=pl.ANY)
    copies = arrays[0].shape[0] + 2
    return pl.pallas_call(
        hand_out_kernel,
        out_shape=tuple(shapes),
        in_specs=[anywhere] * 3,
        out_specs=(anywhere,) * 3,
        scratch_shapes=[pltpu.VMEM(a.shape, a.dtype) for a in arrays]
        + [pltpu.SemaphoreType.DMA((copies,))] * 2,
    )(*arrays)


def fused_shards(
    adjoint_state,
    buoyancy,
    lame_lambda,
    shear_modulus,
    forward_field,
    traces,
    observed,
    pairs,
    patch_basis,
    patch_ids,
    slot_counts,
    owner_map,
):
    tiles, slabs = lax.axis_size("horiz"), lax.axis_size("depth")
    samples = traces.shape[2]
    n_pairs = pairs.shape[0]
    bins = samples // 2
    phases = np.outer(np.arange(1, bins + 1), np.arange(samples)) % samples
    angles = phases * (2.0 * math.pi / samples)
    table = np.concatenate([np.cos(angles), -np.sin(angles)], axis=0) / math.sqrt(samples)
    vmem = pl.BlockSpec(memory_space=pltpu.VMEM)
    anywhere = pl.BlockSpec(memory_space=pl.ANY)
    f32 = jnp.float32
    dma = pltpu.SemaphoreType.DMA
    return pl.pallas_call(
        functools.partial(fused_kernel, tiles, slabs),
        out_shape=(
            jax.ShapeDtypeStruct(adjoint_state.shape, f32),
            jax.ShapeDtypeStruct(observed.shape, f32),
            jax.ShapeDtypeStruct((1, OWN_CAP, YC), f32),
        ),
        in_specs=[anywhere] * 4 + [vmem] * 9,
        out_specs=(anywhere, vmem, vmem),
        scratch_shapes=[
            pltpu.VMEM((12, LEV + 10, EXT_X, YC), f32),
            pltpu.VMEM((12, 4, 8, YC), f32),
            pltpu.VMEM((12, 4, 8, YC), f32),
            pltpu.VMEM((12, 8, 8, YC), f32),
            pltpu.VMEM((12, 8, 8, YC), f32),
            pltpu.VMEM((tiles, 2 * FREQ, BLK * STN), f32),
            pltpu.VMEM((tiles, 2 * FREQ, BLK * STN), f32),
            pltpu.VMEM((2 * FREQ * BLK, 128), f32),
            pltpu.VMEM((2 * FREQ * BLK, 128), f32),
            pltpu.VMEM((1, n_pairs), f32),
            pltpu.VMEM((tiles * slabs, 1, n_pairs), f32),
            pltpu.VMEM((9, FIRST + ITERS + 2, EXT_X, YC), f32),
            pltpu.VMEM((tiles, OWN_CAP, YC), f32),
            pltpu.VMEM((tiles, OWN_CAP, YC), f32),
            dma((5,)),
            dma((tiles,)),
            dma((tiles,)),
            dma((2, 4)),
            dma((2, 4)),
            dma((2, CHUNKS)),
            dma((2, CHUNKS)),
            dma((2, 2, CHUNKS)),
            dma((2, 2, CHUNKS)),
            dma((tiles,)),
            dma((slabs, tiles)),
            dma((tiles,)),
            dma((tiles,)),
        ],
        compiler_params=pltpu.CompilerParams(collective_id=0, has_side_effects=True),
    )(
        adjoint_state,
        buoyancy[None],
        lame_lambda[None],
        shear_modulus[None],
        forward_field,
        traces.reshape(-1, samples),
        observed,
        pairs.T,
        patch_basis,
        patch_ids,
        slot_counts.reshape(1, 1),
        owner_map.reshape(1, -1),
        jnp.asarray(table, f32),
    )


def fits_fused(tiles, slabs, state, traces, pairs):
    return (
        state[1:] == (LEV, XC, YC)
        and traces == (STN, BLK, 128)
        and tiles * FREQ == 64
        and slabs > 1
        and pairs[0] % 128 == 0
    )


def local_program(*args):
    tiles, slabs = lax.axis_size("horiz"), lax.axis_size("depth")
    if fits_fused(tiles, slabs, args[0].shape, args[5].shape, args[7].shape):
        return hand_out(*fused_shards(*args))
    return shards(*args)


def solution(mesh):
    return jax.shard_map(
        local_program,
        mesh=mesh,
        in_specs=(
            P(None, "depth", "horiz", None),
            P("depth", "horiz", None),
            P("depth", "horiz", None),
            P("depth", "horiz", None),
            P("depth", "horiz", None),
            P("horiz", "depth", None),
            P("depth", None, "horiz", None),
            P(),
            P(None, "horiz"),
            P("horiz", None),
            P("horiz"),
            P(),
        ),
        out_specs=(
            P(None, "depth", "horiz", None),
            P("depth", None, "horiz", None),
            P("depth", "horiz", None),
        ),
        check_vma=False,
    )
```

profile of v0, /device:TPU:0, one launch (start us, length us, event | category | flops | bytes accessed | tf_op | source)
XLA Modules:
  0.0 34.1 jit_solution(12099898287568514561)
XLA Ops:
  1.3 30.8 %shard_map.148 = (f32[9,8,16,128]{3,2,1,0:T(8,128)}, f32[1,2,64,256]{3,2,1,0:T(8,128)}, f32[1,8,128]{2,1,0:T(8,128)}) custom-call(f32[9,8,16,128]{3,2,1,0:T(8,128)} %state_ref.1, f32[1,8,16,128]{3,2,1,0:T(8,128)} %bitcast.9, f32[1,8,16,128]{3,2,1,0:T(8,128)} %bitcast.10, f32[1,8,16,128]{3,2,1,0:T(8,128)} %bitcast.11, f32[8,16,128]{2,1,0:T(8,128)} %forward_ref.1, ...), custom_call_target="tpu_custom_call" | custom-call | tf_op jit(solution)/shard_map/pallas_call | solution.py:911
  32.1 2.0 %shard_map.149 = (f32[9,8,16,128]{3,2,1,0:T(8,128)}, f32[1,2,64,256]{3,2,1,0:T(8,128)}, f32[1,8,128]{2,1,0:T(8,128)}) custom-call(f32[9,8,16,128]{3,2,1,0:T(8,128)} %get-tuple-element.6.refs_0_, f32[1,2,64,256]{3,2,1,0:T(8,128)} %get-tuple-element.7.refs_1_, f32[1,8,128]{2,1,0:T(8,128)} %get-tuple-element.8.refs_2_), custom_call_target="tpu_custom_call" | custom-call | tf_op jit(solution)/shard_map/pallas_call | solution.py:876
where the time goes:
time: 34.3 us; the launch traced here: 34.1 us
  Pallas kernels  32.9 us (96%)
  between operations  1.29 us (4%)
    pallas_call x1, Pallas kernels, fused_shards(): pl.pallas_call(functools.partial(fused_kernel, tiles, slabs), out_shape=(...  30.8 us
    pallas_call x1, Pallas kernels, hand_out(): pl.pallas_call(hand_out_kernel, out_shape=tuple(shapes), in_specs=[anywhe...  2.04 us

commit v1 on v0

--- a/solution.py
+++ b/solution.py
@@ -262,6 +262,10 @@
 EXT_X = XC + 8
 FIRST = 5
 CHUNKS = 6
+EARLY = 3
+WIDE = 2
+ALL_VMEM = 67043328
+SPARE = 2**11
 MESH = pl.DeviceIdType.MESH
 
 
@@ -355,6 +359,18 @@
     buo_ref,
     lam_ref,
     mu_ref,
+    forward_hbm,
+    traces_hbm,
+    observed_hbm,
+    pairs_hbm,
+    basis_hbm,
+    ids_hbm,
+    counts_hbm,
+    owner_hbm,
+    table_hbm,
+    ext,
+    cross_ref,
+    grad_ref,
     forward_ref,
     traces_ref,
     observed_ref,
@@ -364,10 +380,6 @@
     counts_ref,
     owner_ref,
     table_ref,
-    final_ref,
-    cross_ref,
-    grad_ref,
-    ext,
     pack_r,
     pack_l,
     halo_r,
@@ -394,29 +406,65 @@
     part_recv,
     row_send,
     row_recv,
+    far_sem,
 ):
     me = lax.axis_index("horiz")
     depth = lax.axis_index("depth")
     n_pairs = pairs_ref.shape[1]
     own = pl.ds(FIRST, LEV)
     arrays = ((0, 9, state_ref), (9, 1, buo_ref), (10, 1, lam_ref), (11, 1, mu_ref))
-
+    pair_rows = tiles // WIDE
+    row_z, row_y = me // WIDE, lax.rem(me, WIDE)
+
+    barrier = pltpu.get_barrier_semaphore()
+    for d in range(1, slabs):
+        other = {"depth": lax.rem(depth + d, slabs)}
+        pl.semaphore_signal(barrier, inc=1, device_id=other, device_id_type=MESH)
+    for k in range(1, WIDE):
+        other = {"horiz": row_z * WIDE + lax.rem(row_y + k, WIDE)}
+        pl.semaphore_signal(barrier, inc=1, device_id=other, device_id_type=MESH)
+
+    def near_rows(run):
+        for step in (-1, 1):
+
+            @pl.when((row_z + step >= 0) & (row_z + step < pair_rows))
+            def _():
+                run(step)
+
+    def greet(step):
+        for k in range(WIDE):
+            other = {"horiz": (row_z + step) * WIDE + k}
+            pl.semaphore_signal(barrier, inc=1, device_id=other, device_id_type=MESH)
+
+    near_rows(greet)
+
+    smalls = (
+        (traces_hbm, traces_ref),
+        (table_hbm, table_ref),
+        (pairs_hbm, pairs_ref),
+        (basis_hbm, basis_ref),
+        (ids_hbm, ids_ref),
+        (counts_hbm, counts_ref),
+        (owner_hbm, owner_ref),
+        (observed_hbm, observed_ref),
+        (forward_hbm, forward_ref),
+    )
+    small_in = [
+        pltpu.make_async_copy(src, dst, local_sem.at[4 + n]) for n, (src, dst) in enumerate(smalls)
+    ]
     locals_in = [
         pltpu.make_async_copy(
             src, ext.at[pl.ds(start, count), own, pl.ds(0, XC)], local_sem.at[n]
         )
         for n, (start, count, src) in enumerate(arrays)
     ]
-    for copy in locals_in:
+    for copy in small_in[:2] + locals_in + small_in[2:]:
         copy.start()
 
-    barrier = pltpu.get_barrier_semaphore()
-    for d in range(slabs):
-        for k in range(tiles):
-            if d or k:
-                other = {"horiz": lax.rem(me + k, tiles), "depth": lax.rem(depth + d, slabs)}
-                pl.semaphore_signal(barrier, inc=1, device_id=other, device_id_type=MESH)
-
+    row = lax.broadcasted_iota(jnp.int32, (8, YC), 0)
+    lower = row < 4
+    for copy in small_in[:2]:
+        copy.wait()
     by_block = jnp.concatenate(
         [traces_ref[pl.ds(b, STN, stride=BLK), :] for b in range(BLK)], axis=0
     )
@@ -427,28 +475,6 @@
             spec_out[t, pl.ds(c * FREQ, FREQ), :] = spectra[
                 c * half + t * FREQ : c * half + (t + 1) * FREQ
             ]
-
-    pl.semaphore_wait(barrier, tiles * slabs - 1)
-
-    spec_copies = []
-    for k in range(1, tiles):
-        peer = lax.rem(me + k, tiles)
-        spec_copies.append(
-            pltpu.make_async_remote_copy(
-                src_ref=spec_out.at[peer],
-                dst_ref=spec_in.at[me],
-                send_sem=spec_send.at[k],
-                recv_sem=spec_recv.at[k],
-                device_id={"horiz": peer},
-                device_id_type=MESH,
-            )
-        )
-    for copy in spec_copies:
-        copy.start()
-    spec_in[me] = spec_out[me]
-
-    row = lax.broadcasted_iota(jnp.int32, (8, YC), 0)
-    lower = row < 4
     for copy in locals_in:
         copy.wait()
 
@@ -510,8 +536,7 @@
     has_left, has_right = me > 0, me < tiles - 1
     has_up, has_down = depth > 0, depth < slabs - 1
 
-    for c in range(CHUNKS):
-
+    def side_start(c):
         @pl.when(has_left)
         def _():
             side_copy(0, c).start()
@@ -520,6 +545,56 @@
         def _():
             side_copy(1, c).start()
 
+    def spec_copy(peer, source):
+        return pltpu.make_async_remote_copy(
+            src_ref=spec_out.at[peer],
+            dst_ref=spec_in.at[source],
+            send_sem=spec_send.at[peer],
+            recv_sem=spec_recv.at[source],
+            device_id={"horiz": peer},
+            device_id_type=MESH,
+        )
+
+    def far_signal(step, stage):
+        pl.semaphore_signal(
+            far_sem.at[(step + 1) // 2, stage],
+            inc=1,
+            device_id={"horiz": me + step * WIDE},
+            device_id_type=MESH,
+        )
+
+    def spec_row(distance):
+        for step in (-1, 1):
+            there = row_z + step * distance
+
+            @pl.when((there >= 0) & (there < pair_rows))
+            def _():
+                for k in range(WIDE):
+                    spec_copy(there * WIDE + k, me).start()
+
+    pl.semaphore_wait(
+        barrier,
+        slabs
+        - 1
+        + WIDE
+        - 1
+        + jnp.where(row_z > 0, WIDE, 0)
+        + jnp.where(row_z < pair_rows - 1, WIDE, 0),
+    )
+    for step in (-1, 1):
+
+        @pl.when(
+            (row_z - step >= 0)
+            & (row_z - step < pair_rows)
+            & (row_z + step >= 0)
+            & (row_z + step < pair_rows)
+        )
+        def _():
+            far_signal(step, 0)
+
+    for c in range(EARLY):
+        side_start(c)
+
     @pl.when(has_up)
     def _():
         for m in range(4):
@@ -529,6 +604,28 @@
     def _():
         for m in range(4):
             slab_copy(1, m).start()
+
+    for k in range(1, WIDE):
+        spec_copy(row_z * WIDE + lax.rem(row_y + k, WIDE), me).start()
+    spec_row(1)
+    for distance in range(2, pair_rows):
+        for step in (-1, 1):
+            source = row_z - step * distance
+            after = row_z + step
+
+            @pl.when((source >= 0) & (source < pair_rows))
+            def _():
+                pl.semaphore_wait(far_sem.at[(step + 1) // 2, distance - 2], 1)
+                if distance < pair_rows - 1:
+
+                    @pl.when((after >= 0) & (after < pair_rows))
+                    def _():
+                        far_signal(step, distance - 1)
+
+        spec_row(distance)
+    for c in range(EARLY, CHUNKS):
+        side_start(c)
+    spec_in[me] = spec_out[me]
 
     def clear_levels(first):
         def clear(a, carry):
@@ -582,6 +679,8 @@
     def _():
         lax.fori_loop(0, 9, clear_added, 0)
 
+    for copy in small_in[2:7]:
+        copy.wait()
     first_pair = pairs_ref[pl.ds(0, 1), :]
     second_pair = pairs_ref[pl.ds(1, 1), :]
     stations = tiles * STN
@@ -609,8 +708,10 @@
     slot_place = dot32(place, named, ((1,), (0,)))
     row_basis = dot32(slot_place, basis_ref[...], ((1,), (0,)))
 
-    for copy in spec_copies:
-        copy.wait_recv()
+    for k in range(1, tiles):
+        source = lax.rem(me + k, tiles)
+        spec_copy(me, source).wait_recv()
+    small_in[7].wait()
     for b in range(BLK):
         wide = jnp.concatenate(
             [spec_in[t][:, b * STN : (b + 1) * STN] for t in range(tiles)], axis=1
@@ -779,10 +880,7 @@
 
         lax.fori_loop(0, 9, add_one, 0)
 
-    final = pltpu.make_async_copy(
-        ext.at[pl.ds(0, 9), own, pl.ds(0, XC)], final_ref, local_sem.at[4]
-    )
-    final.start()
+    small_in[8].wait()
     slab = sum(ext[VZ, FIRST + i, pl.ds(0, XC)] * forward_ref[i] for i in range(LEV))
     rows = dot32(row_basis, slab, ((1,), (0,)))
     for t in range(tiles):
@@ -804,8 +902,8 @@
         copy.start()
     rows_in[me] = rows_out[me]
 
-    for copy in spec_copies:
-        copy.wait_send()
+    for k in range(1, tiles):
+        spec_copy(lax.rem(me + k, tiles), me).wait_send()
 
     @pl.when(has_left)
     def _():
@@ -845,42 +943,41 @@
     grad_ref[0] = sum(rows_in[t] for t in range(tiles))
     for copy in row_copies:
         copy.wait_send()
-    final.wait()
-
-
-def hand_out_kernel(*refs):
-    sources, results, buffers = refs[:3], refs[3:6], refs[6:9]
-    in_sem, out_sem = refs[9:]
-    fields = sources[0].shape[0]
-    moves = [(0, pl.ds(n, 1)) for n in range(fields)] + [(1, pl.ds(0, 1)), (2, pl.ds(0, 1))]
-    reads, writes = [], []
-    for n, (k, some) in enumerate(moves):
-        reads.append(
-            pltpu.make_async_copy(sources[k].at[some], buffers[k].at[some], in_sem.at[n])
-        )
-        writes.append(
-            pltpu.make_async_copy(buffers[k].at[some], results[k].at[some], out_sem.at[n])
-        )
-        reads[-1].start()
-    for read, write in zip(reads, writes):
-        read.wait()
+
+
+def hand_out_kernel(ext, cross, grad, final_ref, cross_ref, grad_ref, out_sem):
+    own = pl.ds(FIRST, LEV)
+    writes = [
+        pltpu.make_async_copy(src, dst, out_sem.at[n])
+        for n, (src, dst) in enumerate(
+            (
+                (ext.at[pl.ds(0, 9), own, pl.ds(0, XC)], final_ref),
+                (cross, cross_ref),
+                (grad, grad_ref),
+            )
+        )
+    ]
+    for write in writes:
         write.start()
     for write in writes:
         write.wait()
 
 
-def hand_out(*arrays):
-    shapes = [jax.ShapeDtypeStruct(a.shape, a.dtype) for a in arrays]
+def hand_out(state, ext, cross, grad):
     anywhere = pl.BlockSpec(memory_space=pl.ANY)
-    copies = arrays[0].shape[0] + 2
+    f32 = jnp.float32
     return pl.pallas_call(
         hand_out_kernel,
-        out_shape=tuple(shapes),
-        in_specs=[anywhere] * 3,
+        out_shape=(
+            jax.ShapeDtypeStruct(state.shape, f32),
+            jax.ShapeDtypeStruct(cross.shape, f32),
+            jax.ShapeDtypeStruct(grad.shape, f32),
+        ),
+        in_specs=[pl.BlockSpec(memory_space=pltpu.VMEM)] * 3,
         out_specs=(anywhere,) * 3,
-        scratch_shapes=[pltpu.VMEM(a.shape, a.dtype) for a in arrays]
-        + [pltpu.SemaphoreType.DMA((copies,))] * 2,
-    )(*arrays)
+        scratch_shapes=[pltpu.SemaphoreType.DMA((3,))],
+        compiler_params=pltpu.CompilerParams(vmem_limit_bytes=2**20),
+    )(ext, cross, grad)
 
 
 def fused_shards(
@@ -908,17 +1005,26 @@
     anywhere = pl.BlockSpec(memory_space=pl.ANY)
     f32 = jnp.float32
     dma = pltpu.SemaphoreType.DMA
+    kept = 4 * (12 * (LEV + 10) * EXT_X * YC + math.prod(observed.shape) + OWN_CAP * YC) + SPARE
     return pl.pallas_call(
         functools.partial(fused_kernel, tiles, slabs),
         out_shape=(
-            jax.ShapeDtypeStruct(adjoint_state.shape, f32),
-            jax.ShapeDtypeStruct(observed.shape, f32),
-            jax.ShapeDtypeStruct((1, OWN_CAP, YC), f32),
+            pltpu.VMEM((12, LEV + 10, EXT_X, YC), f32),
+            pltpu.VMEM(observed.shape, f32),
+            pltpu.VMEM((1, OWN_CAP, YC), f32),
         ),
-        in_specs=[anywhere] * 4 + [vmem] * 9,
-        out_specs=(anywhere, vmem, vmem),
+        in_specs=[anywhere] * 13,
+        out_specs=(vmem, vmem, vmem),
         scratch_shapes=[
-            pltpu.VMEM((12, LEV + 10, EXT_X, YC), f32),
+            pltpu.VMEM(forward_field.shape, f32),
+            pltpu.VMEM((STN * BLK, samples), f32),
+            pltpu.VMEM(observed.shape, f32),
+            pltpu.VMEM((2, n_pairs), jnp.int32),
+            pltpu.VMEM(patch_basis.shape, f32),
+            pltpu.VMEM(patch_ids.shape, jnp.int32),
+            pltpu.VMEM((1, 1), jnp.int32),
+            pltpu.VMEM((1, owner_map.shape[0]), jnp.int32),
+            pltpu.VMEM(table.shape, f32),
             pltpu.VMEM((12, 4, 8, YC), f32),
             pltpu.VMEM((12, 4, 8, YC), f32),
             pltpu.VMEM((12, 8, 8, YC), f32),
@@ -932,7 +1038,7 @@
             pltpu.VMEM((9, FIRST + ITERS + 2, EXT_X, YC), f32),
             pltpu.VMEM((tiles, OWN_CAP, YC), f32),
             pltpu.VMEM((tiles, OWN_CAP, YC), f32),
-            dma((5,)),
+            dma((13,)),
             dma((tiles,)),
             dma((tiles,)),
             dma((2, 4)),
@@ -945,8 +1051,11 @@
             dma((slabs, tiles)),
             dma((tiles,)),
             dma((tiles,)),
+            pltpu.SemaphoreType.REGULAR((2, max(tiles // WIDE - 2, 1))),
         ],
-        compiler_params=pltpu.CompilerParams(collective_id=0, has_side_effects=True),
+        compiler_params=pltpu.CompilerParams(
+            collective_id=0, has_side_effects=True, vmem_limit_bytes=ALL_VMEM - kept
+        ),
     )(
         adjoint_state,
         buoyancy[None],
@@ -977,7 +1086,7 @@
 def local_program(*args):
     tiles, slabs = lax.axis_size("horiz"), lax.axis_size("depth")
     if fits_fused(tiles, slabs, args[0].shape, args[5].shape, args[7].shape):
-        return hand_out(*fused_shards(*args))
+        return hand_out(args[0], *fused_shards(*args))
     return shards(*args)
 
 

time: 34.3 us -> 31.1 us (0.907)
  Pallas kernels: 32.9 us -> 29.5 us
    pallas_call x1, Pallas kernels: 30.8 us -> 28.7 us  [fused_shards(): pl.pallas_call(functools.partial(fused_kernel, tiles, slabs), out_shape=(...]
    pallas_call x1, Pallas kernels: 2.04 us -> 0.88 us  [hand_out(): pl.pallas_call(hand_out_kernel, out_shape=(jax.ShapeDtypeStruct(state.sha...]
where the time goes in v1:
time: 31.1 us; the launch traced here: 30.8 us
  Pallas kernels  29.5 us (95%)
  between operations  1.29 us (4%)
    pallas_call x1, Pallas kernels, fused_shards(): pl.pallas_call(functools.partial(fused_kernel, tiles, slabs), out_shape=(...  28.7 us
    pallas_call x1, Pallas kernels, hand_out(): pl.pallas_call(hand_out_kernel, out_shape=(jax.ShapeDtypeStruct(state.sha...  0.88 us

profile of v1, /device:TPU:0, one launch (start us, length us, event | category | flops | bytes accessed | tf_op | source)
XLA Modules:
  0.0 30.8 jit_solution(16610243135136890410)
XLA Ops:
  1.3 28.7 %shard_map.148 = (f32[12,18,24,128]{3,2,1,0:T(8,128)S(1)}, f32[1,2,64,256]{3,2,1,0:T(8,128)S(1)}, f32[1,8,128]{2,1,0:T(8,128)S(1)}) custom-call(f32[9,8,16,128]{3,2,1,0:T(8,128)} %state_ref.1, f32[1,8,16,128]{3,2,1,0:T(8,128)} %bitcast.9, f32[1,8,16,128]{3,2,1,0:T(8,128)} %bitcast.10, f32[1,8,16,128]{3,2,1,0:T(8,128)} %bitcast.11, ...), custom_call_target="tpu_custom_call" | custom-call | tf_op jit(solution)/shard_map/pallas_call | solution.py:1009
  29.9 0.9 %shard_map.149 = (f32[9,8,16,128]{3,2,1,0:T(8,128)}, f32[1,2,64,256]{3,2,1,0:T(8,128)}, f32[1,8,128]{2,1,0:T(8,128)}) custom-call(f32[12,18,24,128]{3,2,1,0:T(8,128)S(1)} %get-tuple-element.6.ext, f32[1,2,64,256]{3,2,1,0:T(8,128)S(1)} %get-tuple-element.7.cross, f32[1,8,128]{2,1,0:T(8,128)S(1)} %get-tuple-element.8.grad), custom_call_target="tpu_custom_call" | custom-call | tf_op jit(solution)/shard_map/pallas_call | solution.py:969

commit v2 on v1

--- a/solution.py
+++ b/solution.py
@@ -264,6 +264,8 @@
 CHUNKS = 6
 EARLY = 3
 WIDE = 2
+V_LEVELS = 2
+S_LEVELS = 2
 ALL_VMEM = 67043328
 SPARE = 2**11
 MESH = pl.DeviceIdType.MESH
@@ -352,6 +354,18 @@
             ext[k, first + i] = value
 
 
+def in_trips(levels, ext, first, total, count):
+    def body(i, carry):
+        levels(ext, ext, first + count * i, count)
+        return carry
+
+    trips, rest = divmod(total, count)
+    if trips:
+        lax.fori_loop(0, trips, body, 0)
+    if rest:
+        levels(ext, ext, first + count * trips, rest)
+
+
 def fused_kernel(
     tiles,
     slabs,
@@ -368,9 +382,11 @@
     counts_hbm,
     owner_hbm,
     table_hbm,
+    final_out,
+    cross_out,
+    rows_in,
     ext,
     cross_ref,
-    grad_ref,
     forward_ref,
     traces_ref,
     observed_ref,
@@ -392,7 +408,6 @@
     parts,
     added,
     rows_out,
-    rows_in,
     local_sem,
     spec_send,
     spec_recv,
@@ -499,7 +514,7 @@
         return pltpu.make_async_remote_copy(
             src_ref=source.at[some],
             dst_ref=target.at[some, mid_pairs],
-            send_sem=side_send.at[n, c],
+            send_sem=side_send.at[n],
             recv_sem=side_recv.at[n, c],
             device_id={"horiz": me + step},
             device_id_type=MESH,
@@ -515,8 +530,8 @@
         return pltpu.make_async_remote_copy(
             src_ref=source,
             dst_ref=target,
-            send_sem=slab_send.at[n, m],
-            recv_sem=slab_recv.at[n, m],
+            send_sem=slab_send.at[n],
+            recv_sem=slab_recv.at[n],
             device_id={"depth": depth + (-1 if n == 0 else 1)},
             device_id_type=MESH,
         )
@@ -527,10 +542,39 @@
         return pltpu.make_async_remote_copy(
             src_ref=buffer.at[some, pl.ds(2 if n == 0 else 4, 2)],
             dst_ref=buffer.at[some, pl.ds(6 if n == 0 else 0, 2)],
-            send_sem=corner_send.at[n, m, c],
-            recv_sem=corner_recv.at[n, m, c],
+            send_sem=corner_send.at[n, m],
+            recv_sem=corner_recv.at[n, m],
             device_id={"depth": depth + (-1 if n == 0 else 1)},
             device_id_type=MESH,
+        )
+
+    def whole(src, dst, send, recv):
+        return pltpu.make_async_remote_copy(
+            src_ref=src,
+            dst_ref=dst,
+            send_sem=send,
+            recv_sem=recv,
+            device_id={"horiz": me},
+            device_id_type=MESH,
+        )
+
+    def sides(n):
+        source, target = ((pack_r, halo_r), (pack_l, halo_l))[n]
+        return whole(source, target.at[:, mid_pairs], side_send.at[n], side_recv.at[n, 0])
+
+    def slab(n):
+        levels = ext.at[
+            :, pl.ds(FIRST + LEV if n == 0 else FIRST - 4, 4), pl.ds(0, XC)
+        ]
+        return whole(levels, levels, slab_send.at[n], slab_recv.at[n])
+
+    def corners(n, m):
+        buffer = (halo_r, halo_l)[m]
+        return whole(
+            buffer.at[:, pl.ds(2 if n == 0 else 4, 2)],
+            buffer.at[:, pl.ds(6 if n == 0 else 0, 2)],
+            corner_send.at[n, m],
+            corner_recv.at[n, m],
         )
 
     has_left, has_right = me > 0, me < tiles - 1
@@ -549,8 +593,8 @@
         return pltpu.make_async_remote_copy(
             src_ref=spec_out.at[peer],
             dst_ref=spec_in.at[source],
-            send_sem=spec_send.at[peer],
-            recv_sem=spec_recv.at[source],
+            send_sem=spec_send,
+            recv_sem=spec_recv,
             device_id={"horiz": peer},
             device_id_type=MESH,
         )
@@ -708,9 +752,30 @@
     slot_place = dot32(place, named, ((1,), (0,)))
     row_basis = dot32(slot_place, basis_ref[...], ((1,), (0,)))
 
-    for k in range(1, tiles):
-        source = lax.rem(me + k, tiles)
-        spec_copy(me, source).wait_recv()
+    def relay(first, last):
+        for c in range(first, last):
+
+            @pl.when(has_left)
+            def _():
+                side_copy(1, c).wait_recv()
+
+            @pl.when(has_right)
+            def _():
+                side_copy(0, c).wait_recv()
+
+            @pl.when(has_up)
+            def _():
+                for m in range(2):
+                    corner_copy(0, m, c).start()
+
+            @pl.when(has_down)
+            def _():
+                for m in range(2):
+                    corner_copy(1, m, c).start()
+
+    relay(0, EARLY)
+    others = pl.ds(0, tiles - 1)
+    whole(spec_out.at[others], spec_in.at[others], spec_send, spec_recv).wait_recv()
     small_in[7].wait()
     for b in range(BLK):
         wide = jnp.concatenate(
@@ -752,13 +817,13 @@
     terms = weight * (dev_re * dev_re + dev_im * dev_im)
     part[...] = jnp.sum(terms, axis=0, keepdims=True)
 
-    def part_copy(d, k, receiving=False):
-        slot = d * tiles + (lax.rem(me + tiles - k, tiles) if receiving else me)
+    def part_copy(d, k):
+        slot = d * tiles + me
         return pltpu.make_async_remote_copy(
             src_ref=part,
             dst_ref=parts.at[slot],
-            send_sem=part_send.at[k],
-            recv_sem=part_recv.at[d, k],
+            send_sem=part_send,
+            recv_sem=part_recv,
             device_id={"horiz": lax.rem(me + k, tiles), "depth": 0},
             device_id_type=MESH,
         )
@@ -772,26 +837,10 @@
 
     cross_ref[0, 0] = cross_re
     cross_ref[0, 1] = cross_im
-
-    for c in range(CHUNKS):
-
-        @pl.when(has_left)
-        def _():
-            side_copy(1, c).wait_recv()
-
-        @pl.when(has_right)
-        def _():
-            side_copy(0, c).wait_recv()
-
-        @pl.when(has_up)
-        def _():
-            for m in range(2):
-                corner_copy(0, m, c).start()
-
-        @pl.when(has_down)
-        def _():
-            for m in range(2):
-                corner_copy(1, m, c).start()
+    cross_copy = pltpu.make_async_copy(cross_ref, cross_out, local_sem.at[13])
+    cross_copy.start()
+
+    relay(EARLY, CHUNKS)
 
     def unpack(first, count):
         def unpack_one(a, carry):
@@ -807,42 +856,27 @@
 
     @pl.when(has_up)
     def _():
-        for m in range(4):
-            slab_copy(1, m).wait_recv()
+        slab(1).wait_recv()
         for m in range(2):
-            for c in range(CHUNKS):
-                corner_copy(1, m, c).wait_recv()
+            corners(1, m).wait_recv()
 
     @pl.when(has_down)
     def _():
-        for m in range(4):
-            slab_copy(0, m).wait_recv()
+        slab(0).wait_recv()
         for m in range(2):
-            for c in range(CHUNKS):
-                corner_copy(0, m, c).wait_recv()
+            corners(0, m).wait_recv()
 
     unpack(0, 2)
     unpack(6, 2)
 
     for n in range(ITERS):
-
-        def v_body(i, carry):
-            velocity_levels(ext, ext, 1 + n + 2 * i, 2)
-            return carry
-
-        def s_body(i, carry):
-            stress_levels(ext, ext, 2 + n + 2 * i, 2)
-            return carry
-
-        lax.fori_loop(0, 8 - n, v_body, 0)
-        lax.fori_loop(0, 7 - n, s_body, 0)
+        in_trips(velocity_levels, ext, 1 + n, 16 - 2 * n, V_LEVELS)
+        in_trips(stress_levels, ext, 2 + n, 14 - 2 * n, S_LEVELS)
 
     @pl.when(depth == 0)
     def _():
-        for d in range(slabs):
-            for k in range(tiles):
-                if d or k:
-                    part_copy(d, k, True).wait_recv()
+        senders = parts.at[pl.ds(0, tiles * slabs - 1)]
+        whole(senders, senders, part_send, part_recv).wait_recv()
         parts[me] = part[...]
         total = parts[0]
         for t in range(1, tiles * slabs):
@@ -880,9 +914,13 @@
 
         lax.fori_loop(0, 9, add_one, 0)
 
+    final = pltpu.make_async_copy(
+        ext.at[pl.ds(0, 9), own, pl.ds(0, XC)], final_out, local_sem.at[14]
+    )
+    final.start()
     small_in[8].wait()
-    slab = sum(ext[VZ, FIRST + i, pl.ds(0, XC)] * forward_ref[i] for i in range(LEV))
-    rows = dot32(row_basis, slab, ((1,), (0,)))
+    weighted = sum(ext[VZ, FIRST + i, pl.ds(0, XC)] * forward_ref[i] for i in range(LEV))
+    rows = dot32(row_basis, weighted, ((1,), (0,)))
     for t in range(tiles):
         rows_out[t] = rows[t * OWN_CAP : (t + 1) * OWN_CAP]
     row_copies = []
@@ -892,92 +930,91 @@
             pltpu.make_async_remote_copy(
                 src_ref=rows_out.at[peer],
                 dst_ref=rows_in.at[me],
-                send_sem=row_send.at[k],
-                recv_sem=row_recv.at[k],
+                send_sem=row_send,
+                recv_sem=row_recv,
                 device_id={"horiz": peer},
                 device_id_type=MESH,
             )
         )
     for copy in row_copies:
         copy.start()
-    rows_in[me] = rows_out[me]
-
-    for k in range(1, tiles):
-        spec_copy(lax.rem(me + k, tiles), me).wait_send()
+    own_rows = pltpu.make_async_copy(rows_out.at[me], rows_in.at[me], local_sem.at[15])
+    own_rows.start()
+
+    whole(spec_out.at[others], spec_in.at[others], spec_send, spec_recv).wait_send()
 
     @pl.when(has_left)
     def _():
-        for c in range(CHUNKS):
-            side_copy(0, c).wait_send()
+        sides(0).wait_send()
 
     @pl.when(has_right)
     def _():
-        for c in range(CHUNKS):
-            side_copy(1, c).wait_send()
+        sides(1).wait_send()
 
     @pl.when(has_up)
     def _():
-        for m in range(4):
-            slab_copy(0, m).wait_send()
+        slab(0).wait_send()
         for m in range(2):
-            for c in range(CHUNKS):
-                corner_copy(0, m, c).wait_send()
+            corners(0, m).wait_send()
 
     @pl.when(has_down)
     def _():
-        for m in range(4):
-            slab_copy(1, m).wait_send()
+        slab(1).wait_send()
         for m in range(2):
-            for c in range(CHUNKS):
-                corner_copy(1, m, c).wait_send()
-
-    for k in range(1, tiles):
-        part_copy(depth, k).wait_send()
+            corners(1, m).wait_send()
+
+    @pl.when(depth == 0)
+    def _():
+        sent = parts.at[pl.ds(0, tiles - 1)]
+        whole(sent, sent, part_send, part_recv).wait_send()
 
     @pl.when(depth > 0)
     def _():
-        part_copy(depth, 0).wait_send()
-
-    for copy in row_copies:
-        copy.wait_recv()
-    grad_ref[0] = sum(rows_in[t] for t in range(tiles))
-    for copy in row_copies:
-        copy.wait_send()
-
-
-def hand_out_kernel(ext, cross, grad, final_ref, cross_ref, grad_ref, out_sem):
-    own = pl.ds(FIRST, LEV)
+        sent = parts.at[pl.ds(0, tiles)]
+        whole(sent, sent, part_send, part_recv).wait_send()
+
+    all_rows = whole(rows_out.at[others], rows_in.at[others], row_send, row_recv)
+    all_rows.wait_recv()
+    all_rows.wait_send()
+    own_rows.wait()
+    cross_copy.wait()
+    final.wait()
+
+
+def hand_out_kernel(state, cross, rows, state_ref, cross_ref, grad_ref, grad, out_sem):
     writes = [
         pltpu.make_async_copy(src, dst, out_sem.at[n])
         for n, (src, dst) in enumerate(
-            (
-                (ext.at[pl.ds(0, 9), own, pl.ds(0, XC)], final_ref),
-                (cross, cross_ref),
-                (grad, grad_ref),
-            )
+            ((state, state_ref), (cross, cross_ref), (grad, grad_ref))
         )
     ]
-    for write in writes:
-        write.start()
+    writes[0].start()
+    writes[1].start()
+    grad[0] = sum(rows[t] for t in range(rows.shape[0]))
+    writes[2].start()
     for write in writes:
         write.wait()
 
 
-def hand_out(state, ext, cross, grad):
+def hand_out(state, cross, rows):
     anywhere = pl.BlockSpec(memory_space=pl.ANY)
-    f32 = jnp.float32
+    vmem = pl.BlockSpec(memory_space=pltpu.VMEM)
+    grad = jax.ShapeDtypeStruct((1,) + rows.shape[1:], rows.dtype)
     return pl.pallas_call(
         hand_out_kernel,
         out_shape=(
-            jax.ShapeDtypeStruct(state.shape, f32),
-            jax.ShapeDtypeStruct(cross.shape, f32),
-            jax.ShapeDtypeStruct(grad.shape, f32),
+            jax.ShapeDtypeStruct(state.shape, state.dtype),
+            jax.ShapeDtypeStruct(cross.shape, cross.dtype),
+            grad,
         ),
-        in_specs=[pl.BlockSpec(memory_space=pltpu.VMEM)] * 3,
+        in_specs=[anywhere, anywhere, vmem],
         out_specs=(anywhere,) * 3,
-        scratch_shapes=[pltpu.SemaphoreType.DMA((3,))],
+        scratch_shapes=[
+            pltpu.VMEM(grad.shape, grad.dtype),
+            pltpu.SemaphoreType.DMA((3,)),
+        ],
         compiler_params=pltpu.CompilerParams(vmem_limit_bytes=2**20),
-    )(ext, cross, grad)
+    )(state, cross, rows)
 
 
 def fused_shards(
@@ -1001,21 +1038,24 @@
     phases = np.outer(np.arange(1, bins + 1), np.arange(samples)) % samples
     angles = phases * (2.0 * math.pi / samples)
     table = np.concatenate([np.cos(angles), -np.sin(angles)], axis=0) / math.sqrt(samples)
-    vmem = pl.BlockSpec(memory_space=pltpu.VMEM)
     anywhere = pl.BlockSpec(memory_space=pl.ANY)
     f32 = jnp.float32
     dma = pltpu.SemaphoreType.DMA
-    kept = 4 * (12 * (LEV + 10) * EXT_X * YC + math.prod(observed.shape) + OWN_CAP * YC) + SPARE
+    kept = 4 * (
+        math.prod(adjoint_state.shape) + math.prod(observed.shape) + tiles * OWN_CAP * YC
+    )
     return pl.pallas_call(
         functools.partial(fused_kernel, tiles, slabs),
         out_shape=(
+            pltpu.VMEM(adjoint_state.shape, f32),
+            pltpu.VMEM(observed.shape, f32),
+            pltpu.VMEM((tiles, OWN_CAP, YC), f32),
+        ),
+        in_specs=[anywhere] * 13,
+        out_specs=(anywhere, anywhere, anywhere),
+        scratch_shapes=[
             pltpu.VMEM((12, LEV + 10, EXT_X, YC), f32),
             pltpu.VMEM(observed.shape, f32),
-            pltpu.VMEM((1, OWN_CAP, YC), f32),
-        ),
-        in_specs=[anywhere] * 13,
-        out_specs=(vmem, vmem, vmem),
-        scratch_shapes=[
             pltpu.VMEM(forward_field.shape, f32),
             pltpu.VMEM((STN * BLK, samples), f32),
             pltpu.VMEM(observed.shape, f32),
@@ -1037,24 +1077,23 @@
             pltpu.VMEM((tiles * slabs, 1, n_pairs), f32),
             pltpu.VMEM((9, FIRST + ITERS + 2, EXT_X, YC), f32),
             pltpu.VMEM((tiles, OWN_CAP, YC), f32),
-            pltpu.VMEM((tiles, OWN_CAP, YC), f32),
-            dma((13,)),
-            dma((tiles,)),
-            dma((tiles,)),
-            dma((2, 4)),
-            dma((2, 4)),
+            dma((16,)),
+            pltpu.SemaphoreType.DMA(()),
+            pltpu.SemaphoreType.DMA(()),
+            dma((2,)),
+            dma((2,)),
+            dma((2,)),
             dma((2, CHUNKS)),
-            dma((2, CHUNKS)),
-            dma((2, 2, CHUNKS)),
-            dma((2, 2, CHUNKS)),
-            dma((tiles,)),
-            dma((slabs, tiles)),
-            dma((tiles,)),
-            dma((tiles,)),
+            dma((2, 2)),
+            dma((2, 2)),
+            pltpu.SemaphoreType.DMA(()),
+            pltpu.SemaphoreType.DMA(()),
+            pltpu.SemaphoreType.DMA(()),
+            pltpu.SemaphoreType.DMA(()),
             pltpu.SemaphoreType.REGULAR((2, max(tiles // WIDE - 2, 1))),
         ],
         compiler_params=pltpu.CompilerParams(
-            collective_id=0, has_side_effects=True, vmem_limit_bytes=ALL_VMEM - kept
+            collective_id=0, has_side_effects=True, vmem_limit_bytes=ALL_VMEM - kept - SPARE
         ),
     )(
         adjoint_state,
@@ -1086,7 +1125,7 @@
 def local_program(*args):
     tiles, slabs = lax.axis_size("horiz"), lax.axis_size("depth")
     if fits_fused(tiles, slabs, args[0].shape, args[5].shape, args[7].shape):
-        return hand_out(args[0], *fused_shards(*args))
+        return hand_out(*fused_shards(*args))
     return shards(*args)
 
 

time: 31.1 us -> 29.7 us (0.955)
  Pallas kernels: 29.5 us -> 28.2 us
    pallas_call x1, Pallas kernels: 28.7 us -> 27.3 us  [fused_shards(): pl.pallas_call(functools.partial(fused_kernel, tiles, slabs), out_shape=(...]
where the time goes in v2:
time: 29.7 us; the launch traced here: 29.5 us
  Pallas kernels  28.2 us (95%)
  between operations  1.29 us (4%)
    pallas_call x1, Pallas kernels, fused_shards(): pl.pallas_call(functools.partial(fused_kernel, tiles, slabs), out_shape=(...  27.3 us
    pallas_call x1, Pallas kernels, hand_out(): pl.pallas_call(hand_out_kernel, out_shape=(jax.ShapeDtypeStruct(state.sha...  0.88 us

profile of v2, /device:TPU:0, one launch (start us, length us, event | category | flops | bytes accessed | tf_op | source)
XLA Modules:
  0.0 29.5 jit_solution(8720722665499478802)
XLA Ops:
  1.3 27.3 %shard_map.148 = (f32[9,8,16,128]{3,2,1,0:T(8,128)S(1)}, f32[1,2,64,256]{3,2,1,0:T(8,128)S(1)}, f32[8,8,128]{2,1,0:T(8,128)S(1)}) custom-call(f32[9,8,16,128]{3,2,1,0:T(8,128)} %state_ref.1, f32[1,8,16,128]{3,2,1,0:T(8,128)} %bitcast.9, f32[1,8,16,128]{3,2,1,0:T(8,128)} %bitcast.10, f32[1,8,16,128]{3,2,1,0:T(8,128)} %bitcast.11, f32[8,16,128]{2,1,0:T(8,128)} %forward_hbm.1, ...), custom_call_target="tpu_custom_call" | custom-call | tf_op jit(solution)/shard_map/pallas_call | solution.py:1047
  28.6 0.9 %shard_map.149 = (f32[9,8,16,128]{3,2,1,0:T(8,128)}, f32[1,2,64,256]{3,2,1,0:T(8,128)}, f32[1,8,128]{2,1,0:T(8,128)}) custom-call(f32[9,8,16,128]{3,2,1,0:T(8,128)S(1)} %get-tuple-element.6.state, f32[1,2,64,256]{3,2,1,0:T(8,128)S(1)} %get-tuple-element.7.cross, f32[8,8,128]{2,1,0:T(8,128)S(1)} %get-tuple-element.8.rows), custom_call_target="tpu_custom_call" | custom-call | tf_op jit(solution)/shard_map/pallas_call | solution.py:1003

commit v3 on v2

--- a/solution.py
+++ b/solution.py
@@ -264,8 +264,8 @@
 CHUNKS = 6
 EARLY = 3
 WIDE = 2
-V_LEVELS = 2
-S_LEVELS = 2
+V_LEVELS = 16
+S_LEVELS = 14
 ALL_VMEM = 67043328
 SPARE = 2**11
 MESH = pl.DeviceIdType.MESH
@@ -298,7 +298,6 @@
     def behind_y(f):
         return f - jnp.where(lane == 0, 0.0, pltpu.roll(f, 1, 1))
 
-    results = []
     for i in range(count):
         z = first + i
         sxy = ext[SXY, z]
@@ -315,10 +314,8 @@
         vz = ext[VZ, z] + scale * (
             (sxz - roll_x(sxz, False)) + behind_y(syz) + (ext[SZZ, z + 1] - ext[SZZ, z])
         )
-        results.append((vx, vy, vz))
-    for i in range(count):
-        for k, value in zip((VX, VY, VZ), results[i]):
-            ext[k, first + i] = value
+        for k, value in zip((VX, VY, VZ), (vx, vy, vz)):
+            ext[k, z] = value
 
 
 def stress_levels(ext, mats, first, count):
@@ -330,7 +327,6 @@
     def behind_y(f):
         return f - jnp.where(lane == 0, 0.0, pltpu.roll(f, 1, 1))
 
-    results = []
     for i in range(count):
         z = first + i
         vx = ext[VX, z]
@@ -348,10 +344,8 @@
         sxy = ext[SXY, z] + mu * (ahead_y(vx) + (roll_x(vy, True) - vy))
         sxz = ext[SXZ, z] + mu * ((ext[VX, z + 1] - vx) + (roll_x(vz, True) - vz))
         syz = ext[SYZ, z] + mu * ((ext[VY, z + 1] - vy) + ahead_y(vz))
-        results.append((sxx, syy, szz, sxy, sxz, syz))
-    for i in range(count):
-        for k, value in zip((SXX, SYY, SZZ, SXY, SXZ, SYZ), results[i]):
-            ext[k, first + i] = value
+        for k, value in zip((SXX, SYY, SZZ, SXY, SXZ, SYZ), (sxx, syy, szz, sxy, sxz, syz)):
+            ext[k, z] = value
 
 
 def in_trips(levels, ext, first, total, count):
@@ -902,10 +896,8 @@
         added[VZ, FIRST] = deposit
         for n in range(ITERS):
             if n:
-                for z in range(0, n + 1, 2):
-                    velocity_levels(added, ext, FIRST + z, min(2, n + 1 - z))
-            for z in range(0, n + 2, 2):
-                stress_levels(added, ext, FIRST + z, min(2, n + 2 - z))
+                velocity_levels(added, ext, FIRST, n + 1)
+            stress_levels(added, ext, FIRST, n + 2)
 
         def add_one(a, carry):
             for i in range(ITERS + 1):

time: 29.7 us -> 27 us (0.909)
  Pallas kernels: 28.2 us -> 25.5 us
    pallas_call x1, Pallas kernels: 27.3 us -> 24.6 us  [fused_shards(): pl.pallas_call(functools.partial(fused_kernel, tiles, slabs), out_shape=(...]
where the time goes in v3:
time: 27 us; the launch traced here: 26.8 us
  Pallas kernels  25.5 us (94%)
  between operations  1.29 us (5%)
    pallas_call x1, Pallas kernels, fused_shards(): pl.pallas_call(functools.partial(fused_kernel, tiles, slabs), out_shape=(...  24.6 us
    pallas_call x1, Pallas kernels, hand_out(): pl.pallas_call(hand_out_kernel, out_shape=(jax.ShapeDtypeStruct(state.sha...  0.88 us

profile of v3, /device:TPU:0, one launch (start us, length us, event | category | flops | bytes accessed | tf_op | source)
XLA Modules:
  0.0 26.8 jit_solution(18213872515038632339)
XLA Ops:
  1.3 24.6 %shard_map.148 = (f32[9,8,16,128]{3,2,1,0:T(8,128)S(1)}, f32[1,2,64,256]{3,2,1,0:T(8,128)S(1)}, f32[8,8,128]{2,1,0:T(8,128)S(1)}) custom-call(f32[9,8,16,128]{3,2,1,0:T(8,128)} %state_ref.1, f32[1,8,16,128]{3,2,1,0:T(8,128)} %bitcast.9, f32[1,8,16,128]{3,2,1,0:T(8,128)} %bitcast.10, f32[1,8,16,128]{3,2,1,0:T(8,128)} %bitcast.11, f32[8,16,128]{2,1,0:T(8,128)} %forward_hbm.1, ...), custom_call_target="tpu_custom_call" | custom-call | tf_op jit(solution)/shard_map/pallas_call | solution.py:1039
  25.9 0.9 %shard_map.149 = (f32[9,8,16,128]{3,2,1,0:T(8,128)}, f32[1,2,64,256]{3,2,1,0:T(8,128)}, f32[1,8,128]{2,1,0:T(8,128)}) custom-call(f32[9,8,16,128]{3,2,1,0:T(8,128)S(1)} %get-tuple-element.6.state, f32[1,2,64,256]{3,2,1,0:T(8,128)S(1)} %get-tuple-element.7.cross, f32[8,8,128]{2,1,0:T(8,128)S(1)} %get-tuple-element.8.rows), custom_call_target="tpu_custom_call" | custom-call | tf_op jit(solution)/shard_map/pallas_call | solution.py:995
